TPU v7x, 256 devices: a whole 4x4x8 slice. The times are simulated.
256 devices in a mesh: mod: 2 (over core), seq: 8 (over z), tp: 16 (over x, y).
Axes of the slice: x: 4, y: 4, z: 8, core: 2. Of those that a mesh axis runs over, the one named last changes fastest.
Arguments:
- tokens: bfloat16 [8192, 4096], P(('mod', 'seq'), 'tp'), may hold values from -6 to 6
- modality: int32 [8192], replicated, may hold values from 0 to 1, as said below
- norm_gain: float32 [2, 4096], replicated, may hold values from 0.1 to 1.9
- input_weight: bfloat16 [2, 4096, 3, 4096], P('mod', None, None, 'tp'), may hold values from -0.09375 to 0.09375
- head_gain: float32 [2, 2, 128], replicated, may hold values from 1 to 2
- output_weight: bfloat16 [2, 4096, 4096], P('mod', 'tp'), may hold values from -0.125 to 0.125
Outputs:
- update: bfloat16 [8192, 4096], P(('mod', 'seq'), 'tp')
Inputs may be any that keep to these rules, and one draw needn't show every extreme that they name: Each value is constant over aligned spans of 64 tokens. Each token shard (the 512 tokens of one index of mod+seq) holds between 3 and 5 image spans, so at most 320 tokens of either modality. In every draw, for some index of seq both of its token shards hold 320 text tokens, and for another index of seq both hold 320 image tokens.
All inputs are finite; a program needn't handle non-finite values.
Results may differ from a plain program's by a relative error of at most 0.019.
Values may be sent and summed in bfloat16 or wider, within the bound.
A program may use at most 192 MiB of HBM per device.

v0:
```python
from functools import partial
import math
import jax
import jax.numpy as jnp
from jax import lax
from jax.sharding import PartitionSpec as P

HD = 128
CAP = 320
epsilon = 1e-05
sentinel = 1 << 30


def route_table(shard_ids, shard_index, slot_count):
    length = shard_ids.shape[0]
    order = jnp.argsort(shard_ids, stable=True)
    text_count = jnp.sum((shard_ids == 0).astype(jnp.int32))
    padded = jnp.concatenate([order, jnp.zeros((slot_count,), jnp.int32)])
    slot_index = jnp.arange(slot_count, dtype=jnp.int32)
    picked = jnp.stack(
        [padded[:slot_count], lax.dynamic_slice_in_dim(padded, text_count, slot_count)]
    )
    live = jnp.stack([slot_index < text_count, slot_index < length - text_count])
    place = shard_index * length + picked
    query_place = jnp.where(live, place, -1)
    key_place = jnp.where(live, place, sentinel)
    return (order, text_count, picked, live, query_place, key_place)


def select_rows(table, picked, live):
    return jnp.where(live[:, :, None], table[picked], jnp.zeros((), table.dtype))


def head_norm(part, gain):
    return part * lax.rsqrt(jnp.mean(part * part, axis=-1, keepdims=True) + epsilon) * gain


def body(tokens, modality, norm_gain, input_weight, head_gain, output_weight):
    length = tokens.shape[0]
    mod_count = lax.axis_size("mod")
    seq_count = lax.axis_size("seq")
    shards = mod_count * seq_count
    mine = lax.axis_index("mod")
    seq_index = lax.axis_index("seq")
    all_ids = modality.reshape(shards, length)
    own_index = mine * seq_count + seq_index
    own_ids = lax.dynamic_index_in_dim(all_ids, own_index, 0, keepdims=False)
    own_table = route_table(own_ids, own_index, CAP)
    order = own_table[0]
    text_count = own_table[1]
    picked = own_table[2]
    live = own_table[3]
    tables = jax.vmap(partial(route_table, slot_count=CAP))(
        all_ids, jnp.arange(shards, dtype=jnp.int32)
    )
    query_grid = tables[4].reshape(mod_count, seq_count, 2, CAP)
    own_query = lax.dynamic_index_in_dim(query_grid, seq_index, 1, keepdims=False)
    own_query = lax.dynamic_index_in_dim(own_query, mine, 1, keepdims=False).reshape(
        mod_count * CAP
    )
    key_grid = tables[5].reshape(mod_count, seq_count, 2, CAP)
    key_order = jnp.transpose(key_grid, (2, 1, 0, 3)).reshape(shards * mod_count * CAP)
    gathered = lax.all_gather(tokens, "tp", axis=1, tiled=True)
    arrived = lax.all_to_all(
        select_rows(gathered, picked, live), "mod", split_axis=0, concat_axis=0, tiled=True
    )
    rows_total = arrived.shape[0] * arrived.shape[1]
    width = arrived.shape[2]
    states = arrived.reshape(rows_total, width).astype(jnp.float32)
    gain = lax.dynamic_index_in_dim(norm_gain, mine, 0, keepdims=False)
    normed = (
        states * lax.rsqrt(jnp.mean(states * states, axis=1, keepdims=True) + epsilon) * gain
    ).astype(jnp.bfloat16)
    local_width = input_weight.shape[3]
    heads_here = local_width // HD
    projected = jnp.dot(
        normed, input_weight[0].reshape(width, 3 * local_width), preferred_element_type=jnp.float32
    )
    projected = projected.reshape(rows_total, 3, heads_here, HD)
    gains = lax.dynamic_index_in_dim(head_gain, mine, 0, keepdims=False)
    query_rows = head_norm(projected[:, 0], gains[0]).astype(jnp.bfloat16)
    key_rows = (
        head_norm(projected[:, 1], gains[1]).astype(jnp.bfloat16).reshape(rows_total, local_width)
    )
    value_rows = projected[:, 2].astype(jnp.bfloat16).reshape(rows_total, local_width)
    scale = 1.0 / math.sqrt(HD)
    key_piece = lax.all_gather(key_rows, ("mod", "seq"), axis=0, tiled=True)
    value_piece = lax.all_gather(value_rows, ("mod", "seq"), axis=0, tiled=True)
    count = key_piece.shape[0]
    scores = (
        jnp.einsum(
            "rhe,khe->hrk",
            query_rows,
            key_piece.reshape(count, heads_here, HD),
            preferred_element_type=jnp.float32,
        )
        * scale
    )
    weights = jnp.where(key_order[None, None, :] <= own_query[None, :, None], jnp.exp(scores), 0.0)
    totals = jnp.sum(weights, axis=2)
    rounded = weights.astype(jnp.bfloat16)
    weighted = jnp.einsum(
        "hrk,khe->rhe",
        rounded,
        value_piece.reshape(count, heads_here, HD),
        preferred_element_type=jnp.float32,
    )
    weighted, totals = (weighted, totals)
    totals = jnp.where(own_query[None, :] >= 0, totals, 1.0)
    attention = (
        (weighted / jnp.transpose(totals)[:, :, None])
        .astype(jnp.bfloat16)
        .reshape(rows_total, local_width)
    )
    head_terms = jnp.dot(attention, output_weight[0], preferred_element_type=jnp.float32)
    summed = lax.psum_scatter(
        head_terms.astype(jnp.bfloat16), "tp", scatter_dimension=1, tiled=True
    ).astype(jnp.float32)
    result = summed.astype(jnp.bfloat16).reshape(mod_count, CAP, summed.shape[1])
    returned = lax.all_to_all(result, "mod", split_axis=0, concat_axis=0, tiled=True)
    flat = returned.reshape(mod_count * CAP, summed.shape[1])
    inverse = jnp.zeros((length,), jnp.int32).at[order].set(jnp.arange(length, dtype=jnp.int32))
    slot = own_ids * CAP + inverse - own_ids * text_count
    return flat[slot]


def solution(mesh):
    in_specs = (
        P(("mod", "seq"), "tp"),
        P(),
        P(),
        P("mod", None, None, "tp"),
        P(),
        P("mod", "tp", None),
    )
    out_specs = P(("mod", "seq"), "tp")
    return jax.shard_map(body, mesh=mesh, in_specs=in_specs, out_specs=out_specs, check_vma=False)
```

profile of v0, /device:TPU:1, one launch (start us, length us, event | category | flops | bytes accessed | tf_op | source)
XLA Modules:
  0.0 324.6 jit_solution(6976612528921012147)
XLA Ops:
  7.4 0.7 all-gather.4.cloned.1.call-update
  8.1 1.4 reshape.304
  9.5 0.6 broadcast_in_dim.70
  10.2 0.7 constant_dynamic-slice_fusion.3
  10.9 0.7 convert_reduce_fusion.1
  12.9 3.8 %sort.34 = (s32[512]{0:T(512)}, s32[512]{0:T(512)S(1)}) sort(s32[512]{0:T(512)S(1)} %bitcast.92, s32[512]{0:T(512)S(1)} %iota.35), dimensions={0}, to_apply=%region_1.2 | sort | flops 4608 | bytes 8192 | tf_op jit(solution)/shard_map/jit(argsort)/sort | solution.py:16
  18.2 0.6 iota_compare_fusion.2
  18.8 8.8 %copy.12 = bf16[1,4096,3,256]{1,3,2,0:T(8,128)(2,1)} copy(bf16[1,4096,3,256]{3,1,2,0:T(8,128)(2,1)} %param.9) | data formatting | bytes 12582912 | tf_op args[3]
  27.7 48.4 %all-gather.4.cloned.1.call-done = bf16[512,4096]{1,0:T(8,128)(2,1)} async-done(((bf16[512,256]{1,0:T(8,128)(2,1)}), bf16[512,4096]{1,0:T(8,128)(2,1)}) %all-gather.4.cloned.1.call-update) | async-done | bytes 4194320 | tf_op jit(solution)/shard_map/all_gather | solution.py:63
  76.1 14.3 %gather_fusion = bf16[640,4096]{1,0:T(8,128)(2,1)} fusion(bf16[512,4096]{1,0:T(8,128)(2,1)} %all-gather.4.cloned.1.call-done, s32[1024]{0:T(1024)S(1)} %pad_clamp_fusion.1), kind=kCustom, calls=%fused_computation | custom fusion | bytes 10488320 | tf_op jit(solution)/shard_map/gather | solution.py:31
  90.5 2.9 broadcast_select_fusion
  93.4 9.2 %all_to_all.10 = bf16[2,320,4096]{2,1,0:T(8,128)(2,1)S(1)} all-to-all(bf16[2,320,4096]{2,1,0:T(8,128)(2,1)S(1)} %broadcast_select_fusion), channel_id=1, replica_groups=mesh['mod'=2,'seq'=8,'tp'=16] {'mod'}, dimensions={0} | all-to-all | bytes 10485760 | tf_op jit(solution)/shard_map/all_to_all | solution.py:64
  102.6 1.1 fusion.5
  103.7 2.1 fusion.7
  105.8 5.1 %fusion.29 = f32[640,3,2,128]{0,3,2,1:T(8,128)S(1)} fusion(bf16[640,4096,1,1]{1,0,3,2:T(8,128)(2,1)S(1)} %bitcast.85, bf16[3,2,128,4096]{3,2,1,0:T(8,128)(2,1)S(1)} %bitcast.84), kind=kOutput, calls=%fused_computation.75 | convolution fusion | flops 4026531840 | bytes 13500416 | tf_op jit(solution)/shard_map/dot_general | solution.py:76
  110.9 1.3 copy-done.1
  112.3 0.8 fusion.19
  113.5 0.8 concatenate.26
  114.3 0.7 slice_bitcast_fusion.1
  115.0 1.8 slice.59
  117.2 30.9 %while.1 = (s32[]{:T(128)}, s32[16,832]{1,0:T(8,128)S(1)}, s32[16,2]{0,1:T(2,128)S(1)}, s32[16,320]{1,0:T(8,128)S(1)}, s32[]{:T(128)}, /*index=5*/s32[]{:T(128)}) while((s32[]{:T(128)}, s32[16,832]{1,0:T(8,128)S(1)}, s32[16,2]{0,1:T(2,128)S(1)}, s32[16,320]{1,0:T(8,128)S(1)}, s32[]{:T(128)}, /*index=5*/s32[]{:T(128)}) %tuple.26), condition=%wide.while_cond, body=%wide.while_body.sunk | while | flops 2 | bytes 5233 | solution.py:21
  117.8 1.3 dynamic-slice.9
  119.7 1.3 dynamic-slice.9
  121.6 1.3 dynamic-slice.9
  123.6 1.3 dynamic-slice.9
  125.5 1.3 dynamic-slice.9
  127.4 1.3 dynamic-slice.9
  129.4 1.3 dynamic-slice.9
  131.3 1.3 dynamic-slice.9
  133.2 1.3 dynamic-slice.9
  135.2 1.3 dynamic-slice.9
  137.1 1.3 dynamic-slice.9
  139.0 1.3 dynamic-slice.9
  140.9 1.3 dynamic-slice.9
  142.9 1.3 dynamic-slice.9
  144.8 1.3 dynamic-slice.9
  146.7 1.3 dynamic-slice.9
  148.4 6.8 %broadcast_compare_fusion = pred[640,10240]{1,0:T(8,128)(4,1)} fusion(s32[10240]{0:T(1024)S(1)} %le.22, s32[640]{0:T(1024)S(1)} %le.24), kind=kLoop, calls=%fused_computation.9 | loop fusion | flops 6553600 | bytes 6597120 | tf_op jit(solution)/shard_map/le | solution.py:99
  155.2 1.2 multiply_reduce_fusion.1
  156.5 26.4 %fusion = (f32[2,640]{1,0:T(2,128)S(1)}, f32[2,640,10240]{2,1,0:T(8,128)}) fusion(pred[640,10240]{1,0:T(8,128)(4,1)} %broadcast_compare_fusion, bf16[10240,2,128]{0,2,1:T(8,128)(2,1)} %bitcast.95, f32[640,3,2,128]{0,3,2,1:T(8,128)} %copy-done.1, f32[128]{0:T(128)S(1)} %get-tuple-element.33, f32[640,2]{0,1:T(2,128)S(1)} %add_rsqrt_fusion.1), kind=kOutput, calls=%fused_computation.5 | convolution fusion | flops 3395255040 | bytes 64891392 | tf_op jit(solution)/shard_map/rhe,khe->hrk/dot_general | solution.py:91
  182.9 18.0 %all-gather.6.cloned.1.call-done = bf16[10240,256]{0,1:T(8,128)(2,1)} async-done(((bf16[640,256]{0,1:T(8,128)(2,1)}), bf16[10240,256]{0,1:T(8,128)(2,1)}) %all-gather.6.cloned.1.call-update) | async-done | bytes 5242896 | tf_op jit(solution)/shard_map/all_gather | solution.py:88
  200.9 22.6 %fusion.15 = bf16[640,2,128]{0,2,1:T(8,128)(2,1)S(1)} fusion(bf16[10240,2,128]{0,2,1:T(8,128)(2,1)} %bitcast.96, f32[2,640,10240]{2,1,0:T(8,128)} %get-tuple-element.36, pred[640,10240]{1,0:T(8,128)(4,1)} %broadcast_compare_fusion, f32[640,2]{0,1:T(2,128)S(1)} %select_bitcast_fusion.2), kind=kOutput, calls=%fused_computation.20 | convolution fusion | flops 3395092480 | bytes 64558080 | tf_op jit(solution)/shard_map/hrk,khe->rhe/dot_general | solution.py:102
  223.5 3.9 %convolution_convert_fusion = bf16[640,4096]{1,0:T(8,128)(2,1)} fusion(bf16[640,256]{0,1:T(8,128)(2,1)S(1)} %bitcast.87, bf16[1,256,4096]{2,1,0:T(8,128)(2,1)S(1)} %copy-done), kind=kOutput, calls=%fused_computation.15 | convolution fusion | flops 1344798720 | bytes 7667712 | tf_op jit(solution)/shard_map/dot_general | solution.py:115
  227.4 2.4 scatter_custom_fusion
  229.9 0.6 compare_select_fusion.1
  230.5 77.9 %reduce-scatter.2.cloned.1.call-done = bf16[640,256]{1,0:T(8,128)(2,1)} async-done(((bf16[640,4096]{1,0:T(8,128)(2,1)}), bf16[640,256]{1,0:T(8,128)(2,1)}) %reduce-scatter.2.cloned.1.call-update) | async-done | bytes 327696 | tf_op jit(solution)/shard_map/reduce_scatter | solution.py:116
  308.5 6.4 %all_to_all.11 = bf16[2,320,256]{2,1,0:T(8,128)(2,1)S(1)} all-to-all(bf16[2,320,256]{2,1,0:T(8,128)(2,1)} %bitcast.88), channel_id=1, replica_groups=mesh['mod'=2,'seq'=8,'tp'=16] {'mod'}, dimensions={0} | all-to-all | bytes 655360 | tf_op jit(solution)/shard_map/all_to_all | solution.py:120
  314.9 2.6 gather_fusion.1
  (107 shorter events, 11.5 us)
Async XLA Ops:
  7.4 216.1 %copy-start = (bf16[1,256,4096]{2,1,0:T(8,128)(2,1)S(1)}, bf16[1,256,4096]{2,1,0:T(8,128)(2,1)}, u32[]{:S(2)}) copy-start(bf16[1,256,4096]{2,1,0:T(8,128)(2,1)} %param.11) | copy-start | bytes 6291460
  7.4 68.8 %all-gather.4.cloned.1.call-start = ((), (), s32[]{:S(2)}) async-start(), calls=%async_computation.3 | async-start | bytes 4456448 | tf_op jit(solution)/shard_map/all_gather | solution.py:63
  8.1 105.4 %sort.37.cloned.1.call-start = ((), (), s32[]{:S(2)}) async-start(), calls=%async_computation.7 | async-start | bytes 196640 | tf_op jit(solution)/shard_map/vmap(jit(argsort))/sort | solution.py:16
  10.2 146.4 %all-gather.8.cloned.1.call-start = ((), (), s32[]{:S(2)}) async-start(), calls=%async_computation.5 | async-start | bytes 5570560 | tf_op jit(solution)/shard_map/all_gather | solution.py:87
  18.8 8.8 %copy-start.3 = (f32[2,4096]{1,0:T(2,128)S(1)}, f32[2,4096]{1,0:T(2,128)}, u32[]{:S(2)}) copy-start(f32[2,4096]{1,0:T(2,128)} %param.8) | copy-start | bytes 98308
  18.8 8.8 %copy-start.4 = (f32[2,2,128]{2,1,0:T(2,128)S(1)}, f32[2,2,128]{2,1,0:T(2,128)}, u32[]{:S(2)}) copy-start(f32[2,2,128]{2,1,0:T(2,128)} %param.10) | copy-start | bytes 6148
  102.6 3.3 %slice-start = ((s8[6291456]{0:T(1024)(128)(4,1)}), s8[4194304]{0:T(1024)(128)(4,1)S(1)}, s32[]{:S(2)}) async-start(s8[6291456]{0:T(1024)(128)(4,1)} %bitcast.82), calls=%async_computation.9 | async-start | bytes 8388608
  103.7 2.1 slice-start.1
  105.8 7.4 %copy-start.2 = (s32[16,512]{1,0:T(8,128)S(1)}, s32[16,512]{1,0:T(8,128)}, u32[]{:S(2)}) copy-start(s32[16,512]{1,0:T(8,128)} %reshape.304) | copy-start | bytes 98308
  110.9 1.3 copy-start.1
  113.2 87.7 %all-gather.6.cloned.1.call-start = ((), (), s32[]{:S(2)}) async-start(), calls=%async_computation.4 | async-start | bytes 5570560 | tf_op jit(solution)/shard_map/all_gather | solution.py:88
  116.9 191.6 %reduce-scatter.2.cloned.1.call-start = ((), (), s32[]{:S(2)}) async-start(), calls=%async_computation.6 | async-start | bytes 5570560 | tf_op jit(solution)/shard_map/reduce_scatter | solution.py:116
Sparse Core Ops, SparseCore 0:
  10.6 65.4 all-gather.3
  113.3 43.1 all-gather.7
  158.3 42.5 all-gather.5
  227.5 80.8 reduce-scatter.1
Sparse Core Ops, SparseCore 1:
  11.0 2.4 sort.39.cloned.1.call-done
  (1 shorter events, 0.0 us)
where the time goes:
time: 326 us; the launch traced here: 325 us
  waiting for transfers between devices  145 us (44%)
  local copies, waits for them, and re-layouts  66.6 us (20%)
  matrix products  57.9 us (18%)
  other arithmetic  21.1 us (6%)
  between operations  17.4 us (5%)
  blocking collectives  15.6 us (5%)
    reduce_scatter x1, waiting for transfers between devices, body(): lax.psum_scatter(head_terms.astype(jnp.bfloat16), 'tp', scatter_dimension...  77.9 us
    all_gather x1, waiting for transfers between devices, body(): gathered = lax.all_gather(tokens, 'tp', axis=1, tiled=True)  48.4 us
    gather x64, local copies, waits for them, and re-layouts  30.5 us
    dot_general x1, matrix products, body(): jnp.einsum('rhe,khe->hrk', query_rows, key_piece.reshape(count, heads_her...  26.4 us
    dot_general x1, matrix products, body(): jnp.einsum('hrk,khe->rhe', rounded, value_piece.reshape(count, heads_here...  22.6 us
    all_gather x1, waiting for transfers between devices, body(): value_piece = lax.all_gather(value_rows, ('mod', 'seq'), axis=0, tiled=True)  18 us
    gather x1, local copies, waits for them, and re-layouts, select_rows(): table[picked]  14.3 us
    unnamed x18, local copies, waits for them, and re-layouts  10.2 us
  transfers between devices with their start and end apart: 4, of which 4 were waited for; matrix products, arithmetic and copies ran while one was open for 27% of the time, Pallas kernels for 0%

commit v1 on v0

--- a/solution.py
+++ b/solution.py
@@ -36,6 +36,12 @@
 
 
 def body(tokens, modality, norm_gain, input_weight, head_gain, output_weight):
+
+    def _create_sides(view):
+        total_devices = lax.axis_size("tp")
+        log = [total_devices if p == 1 else 1 for p in range(view.ndim)]
+        return lax.all_to_all(jnp.tile(view, log), "tp", split_axis=1, concat_axis=1, tiled=True)
+
     length = tokens.shape[0]
     mod_count = lax.axis_size("mod")
     seq_count = lax.axis_size("seq")
@@ -60,7 +66,7 @@
     )
     key_grid = tables[5].reshape(mod_count, seq_count, 2, CAP)
     key_order = jnp.transpose(key_grid, (2, 1, 0, 3)).reshape(shards * mod_count * CAP)
-    gathered = lax.all_gather(tokens, "tp", axis=1, tiled=True)
+    gathered = _create_sides(tokens)
     arrived = lax.all_to_all(
         select_rows(gathered, picked, live), "mod", split_axis=0, concat_axis=0, tiled=True
     )

time: 326 us -> 343 us (1.052)
  starting transfers between devices: 0.35 us -> 8.12 us
  local copies, waits for them, and re-layouts: 66.6 us -> 74.2 us
    all_gather x1 -> x0, waiting for transfers between devices: 48.4 us -> none  [body(): gathered = lax.all_gather(tokens, 'tp', axis=1, tiled=True)]
    all_to_all x0 -> x1, waiting for transfers between devices: none -> 42.6 us  [_create_sides(): lax.all_to_all(jnp.tile(view, log), 'tp', split_axis=1, concat_axis=1, ti...]
    all_to_all x0 -> x1, starting transfers between devices: none -> 7.77 us  [_create_sides(): lax.all_to_all(jnp.tile(view, log), 'tp', split_axis=1, concat_axis=1, ti...]
    all_gather x1, waiting for transfers between devices: 0.12 us -> 7.35 us  [body(): key_piece = lax.all_gather(key_rows, ('mod', 'seq'), axis=0, tiled=True)]
    all_to_all x0 -> x1, local copies, waits for them, and re-layouts: none -> 4.79 us  [_create_sides(): lax.all_to_all(jnp.tile(view, log), 'tp', split_axis=1, concat_axis=1, ti...]
    another operation x0 -> x1, local copies, waits for them, and re-layouts: none -> 3.58 us  [_create_sides(): jnp.tile(view, log)]
    unnamed x18 -> x20, local copies, waits for them, and re-layouts: 10.2 us -> 10.2 us
  transfers between devices with their start and end apart: 4 -> 4, of which waited for: 4 -> 4; matrix products, arithmetic and copies ran while one was open for 27% -> 26% of each run, Pallas kernels for 0% -> 0%
where the time goes in v1:
time: 343 us; the launch traced here: 341 us
  waiting for transfers between devices  145 us (42%)
  local copies, waits for them, and re-layouts  74.2 us (22%)
  matrix products  57.9 us (17%)
  other arithmetic  21.1 us (6%)
  between operations  17.7 us (5%)
  blocking collectives  16.5 us (5%)
  starting transfers between devices  8.12 us (2%)
    reduce_scatter x1, waiting for transfers between devices, body(): lax.psum_scatter(head_terms.astype(jnp.bfloat16), 'tp', scatter_dimension...  77.7 us
    all_to_all x1, waiting for transfers between devices, _create_sides(): lax.all_to_all(jnp.tile(view, log), 'tp', split_axis=1, concat_axis=1, ti...  42.6 us
    gather x64, local copies, waits for them, and re-layouts  30.5 us
    dot_general x1, matrix products, body(): jnp.einsum('rhe,khe->hrk', query_rows, key_piece.reshape(count, heads_her...  26.4 us
    dot_general x1, matrix products, body(): jnp.einsum('hrk,khe->rhe', rounded, value_piece.reshape(count, heads_here...  22.6 us
    all_gather x1, waiting for transfers between devices, body(): value_piece = lax.all_gather(value_rows, ('mod', 'seq'), axis=0, tiled=True)  17.7 us
    gather x1, local copies, waits for them, and re-layouts, select_rows(): table[picked]  14.3 us
    unnamed x20, local copies, waits for them, and re-layouts  10.2 us
  transfers between devices with their start and end apart: 4, of which 4 were waited for; matrix products, arithmetic and copies ran while one was open for 26% of the time, Pallas kernels for 0%

profile of v1, /device:TPU:1, one launch (start us, length us, event | category | flops | bytes accessed | tf_op | source)
XLA Modules:
  0.0 341.3 jit_solution(4793576755810268711)
XLA Ops:
  7.4 3.6 %tile.2 = bf16[512,16,256]{2,0,1:T(8,128)(2,1)} broadcast(bf16[512,256]{1,0:T(8,128)(2,1)} %param.6), dimensions={0,2} | broadcast | bytes 4456448 | tf_op jit(solution)/shard_map/tile | solution.py:43
  11.0 7.8 %all-to-all-start = ((bf16[512,16,256]{2,0,1:T(8,128)(2,1)}), bf16[512,16,256]{2,0,1:T(8,128)(2,1)}, u32[]{:S(2)}, u32[]{:S(2)}) async-start(bf16[512,16,256]{2,0,1:T(8,128)(2,1)} %tile.2), calls=%async_computation | async-start | bytes 8388608 | tf_op jit(solution)/shard_map/all_to_all | solution.py:43
  20.1 0.7 constant_dynamic-slice_fusion.3
  20.8 0.7 convert_reduce_fusion.1
  22.8 3.8 %sort.34 = (s32[512]{0:T(512)}, s32[512]{0:T(512)S(1)}) sort(s32[512]{0:T(512)S(1)} %bitcast.95, s32[512]{0:T(512)S(1)} %iota.35), dimensions={0}, to_apply=%region_1.2 | sort | flops 4608 | bytes 8192 | tf_op jit(solution)/shard_map/jit(argsort)/sort | solution.py:16
  28.1 8.8 %copy.18 = bf16[1,4096,3,256]{1,3,2,0:T(8,128)(2,1)} copy(bf16[1,4096,3,256]{3,1,2,0:T(8,128)(2,1)} %param.9) | data formatting | bytes 12582912 | tf_op args[3]
  36.9 0.6 iota_compare_fusion.2
  37.6 42.6 %all-to-all-done = bf16[512,16,256]{2,0,1:T(8,128)(2,1)} async-done(((bf16[512,16,256]{2,0,1:T(8,128)(2,1)}), bf16[512,16,256]{2,0,1:T(8,128)(2,1)}, u32[]{:S(2)}, u32[]{:S(2)}) %all-to-all-start) | async-done | bytes 4194336 | tf_op jit(solution)/shard_map/all_to_all | solution.py:43
  80.2 4.8 %copy.25 = bf16[16,64,8,256]{3,2,0,1:T(8,128)(2,1)} copy(bf16[16,64,8,256]{3,2,1,0:T(8,128)(2,1)} %bitcast.40) | data formatting | bytes 8388608 | tf_op jit(solution)/shard_map/all_to_all | solution.py:43
  85.0 14.3 %gather_fusion = bf16[640,4096]{1,0:T(8,128)(2,1)} fusion(bf16[512,4096]{1,0:T(8,128)(2,1)} %bitcast.82, s32[1024]{0:T(1024)S(1)} %pad_clamp_fusion.1), kind=kCustom, calls=%fused_computation | custom fusion | bytes 10488320 | tf_op jit(solution)/shard_map/gather | solution.py:31
  99.4 2.9 broadcast_select_fusion
  102.3 10.0 %all_to_all.19 = bf16[2,320,4096]{2,1,0:T(8,128)(2,1)S(1)} all-to-all(bf16[2,320,4096]{2,1,0:T(8,128)(2,1)S(1)} %broadcast_select_fusion), channel_id=1, replica_groups=mesh['mod'=2,'seq'=8,'tp'=16] {'mod'}, dimensions={0} | all-to-all | bytes 10485760 | tf_op jit(solution)/shard_map/all_to_all | solution.py:70
  112.3 1.1 fusion.5
  113.4 2.1 fusion.7
  115.6 5.1 %fusion.29 = f32[640,3,2,128]{0,3,2,1:T(8,128)S(1)} fusion(bf16[640,4096,1,1]{1,0,3,2:T(8,128)(2,1)S(1)} %bitcast.88, bf16[3,2,128,4096]{3,2,1,0:T(8,128)(2,1)S(1)} %bitcast.87), kind=kOutput, calls=%fused_computation.75 | convolution fusion | flops 4026531840 | bytes 13500416 | tf_op jit(solution)/shard_map/dot_general | solution.py:82
  120.7 1.3 copy-done.1
  122.1 0.8 fusion.19
  123.3 0.8 concatenate.26
  124.0 0.7 slice_bitcast_fusion.1
  124.8 1.8 slice.59
  126.9 30.9 %while.1 = (s32[]{:T(128)}, s32[16,832]{1,0:T(8,128)S(1)}, s32[16,2]{0,1:T(2,128)S(1)}, s32[16,320]{1,0:T(8,128)S(1)}, s32[]{:T(128)}, /*index=5*/s32[]{:T(128)}) while((s32[]{:T(128)}, s32[16,832]{1,0:T(8,128)S(1)}, s32[16,2]{0,1:T(2,128)S(1)}, s32[16,320]{1,0:T(8,128)S(1)}, s32[]{:T(128)}, /*index=5*/s32[]{:T(128)}) %tuple.26), condition=%wide.while_cond, body=%wide.while_body.sunk | while | flops 2 | bytes 5233 | solution.py:21
  127.5 1.3 dynamic-slice.9
  129.4 1.3 dynamic-slice.9
  131.4 1.3 dynamic-slice.9
  133.3 1.3 dynamic-slice.9
  135.2 1.3 dynamic-slice.9
  137.2 1.3 dynamic-slice.9
  139.1 1.3 dynamic-slice.9
  141.0 1.3 dynamic-slice.9
  142.9 1.3 dynamic-slice.9
  144.9 1.3 dynamic-slice.9
  146.8 1.3 dynamic-slice.9
  148.7 1.3 dynamic-slice.9
  150.7 1.3 dynamic-slice.9
  152.6 1.3 dynamic-slice.9
  154.5 1.3 dynamic-slice.9
  156.4 1.3 dynamic-slice.9
  158.1 6.8 %broadcast_compare_fusion = pred[640,10240]{1,0:T(8,128)(4,1)} fusion(s32[10240]{0:T(1024)S(1)} %le.22, s32[640]{0:T(1024)S(1)} %le.24), kind=kLoop, calls=%fused_computation.9 | loop fusion | flops 6553600 | bytes 6597120 | tf_op jit(solution)/shard_map/le | solution.py:105
  165.0 1.2 multiply_reduce_fusion.1
  166.1 7.3 %all-gather.5.cloned.1.call-done = bf16[10240,256]{0,1:T(8,128)(2,1)} async-done(((bf16[640,256]{0,1:T(8,128)(2,1)}), bf16[10240,256]{0,1:T(8,128)(2,1)}) %all-gather.5.cloned.1.call-update) | async-done | bytes 5242896 | tf_op jit(solution)/shard_map/all_gather | solution.py:93
  173.5 26.4 %fusion = (f32[2,640]{1,0:T(2,128)S(1)}, f32[2,640,10240]{2,1,0:T(8,128)}) fusion(pred[640,10240]{1,0:T(8,128)(4,1)} %broadcast_compare_fusion, bf16[10240,2,128]{0,2,1:T(8,128)(2,1)} %bitcast.98, f32[640,3,2,128]{0,3,2,1:T(8,128)} %copy-done.1, f32[128]{0:T(128)S(1)} %get-tuple-element.33, f32[640,2]{0,1:T(2,128)S(1)} %add_rsqrt_fusion.1), kind=kOutput, calls=%fused_computation.5 | convolution fusion | flops 3395255040 | bytes 64891392 | tf_op jit(solution)/shard_map/rhe,khe->hrk/dot_general | solution.py:97
  199.9 17.7 %all-gather.3.cloned.1.call-done = bf16[10240,256]{0,1:T(8,128)(2,1)} async-done(((bf16[640,256]{0,1:T(8,128)(2,1)}), bf16[10240,256]{0,1:T(8,128)(2,1)}) %all-gather.3.cloned.1.call-update) | async-done | bytes 5242896 | tf_op jit(solution)/shard_map/all_gather | solution.py:94
  217.6 22.6 %fusion.15 = bf16[640,2,128]{0,2,1:T(8,128)(2,1)S(1)} fusion(bf16[10240,2,128]{0,2,1:T(8,128)(2,1)} %bitcast.99, f32[2,640,10240]{2,1,0:T(8,128)} %get-tuple-element.36, pred[640,10240]{1,0:T(8,128)(4,1)} %broadcast_compare_fusion, f32[640,2]{0,1:T(2,128)S(1)} %select_bitcast_fusion.2), kind=kOutput, calls=%fused_computation.20 | convolution fusion | flops 3395092480 | bytes 64558080 | tf_op jit(solution)/shard_map/hrk,khe->rhe/dot_general | solution.py:108
  240.2 3.9 %convolution_convert_fusion = bf16[640,4096]{1,0:T(8,128)(2,1)} fusion(bf16[640,256]{0,1:T(8,128)(2,1)S(1)} %bitcast.90, bf16[1,256,4096]{2,1,0:T(8,128)(2,1)S(1)} %copy-done), kind=kOutput, calls=%fused_computation.15 | convolution fusion | flops 1344798720 | bytes 7667712 | tf_op jit(solution)/shard_map/dot_general | solution.py:121
  244.1 2.4 scatter_custom_fusion
  247.2 77.7 %reduce-scatter.2.cloned.1.call-done = bf16[640,256]{1,0:T(8,128)(2,1)} async-done(((bf16[640,4096]{1,0:T(8,128)(2,1)}), bf16[640,256]{1,0:T(8,128)(2,1)}) %reduce-scatter.2.cloned.1.call-update) | async-done | bytes 327696 | tf_op jit(solution)/shard_map/reduce_scatter | solution.py:122
  324.9 6.4 %all_to_all.20 = bf16[2,320,256]{2,1,0:T(8,128)(2,1)S(1)} all-to-all(bf16[2,320,256]{2,1,0:T(8,128)(2,1)} %bitcast.91), channel_id=1, replica_groups=mesh['mod'=2,'seq'=8,'tp'=16] {'mod'}, dimensions={0} | all-to-all | bytes 655360 | tf_op jit(solution)/shard_map/all_to_all | solution.py:126
  331.3 2.6 gather_fusion.1
  (110 shorter events, 13.3 us)
Async XLA Ops:
  7.4 232.8 %copy-start = (bf16[1,256,4096]{2,1,0:T(8,128)(2,1)S(1)}, bf16[1,256,4096]{2,1,0:T(8,128)(2,1)}, u32[]{:S(2)}) copy-start(bf16[1,256,4096]{2,1,0:T(8,128)(2,1)} %param.11) | copy-start | bytes 6291460
  11.0 7.8 %copy-start.3 = (s32[8192]{0:T(1024)S(1)}, s32[8192]{0:T(1024)}, u32[]{:S(2)}) copy-start(s32[8192]{0:T(1024)} %param.7) | copy-start | bytes 98308
  11.0 69.3 %all-to-all-start = ((bf16[512,16,256]{2,0,1:T(8,128)(2,1)}), bf16[512,16,256]{2,0,1:T(8,128)(2,1)}, u32[]{:S(2)}, u32[]{:S(2)}) async-start(bf16[512,16,256]{2,0,1:T(8,128)(2,1)} %tile.2), calls=%async_computation | async-start | bytes 8388608 | tf_op jit(solution)/shard_map/all_to_all | solution.py:43
  18.7 104.5 %sort.37.cloned.1.call-start = ((), (), s32[]{:S(2)}) async-start(), calls=%async_computation.7 | async-start | bytes 196640 | tf_op jit(solution)/shard_map/vmap(jit(argsort))/sort | solution.py:16
  20.0 153.4 %all-gather.5.cloned.1.call-start = ((), (), s32[]{:S(2)}) async-start(), calls=%async_computation.5 | async-start | bytes 5570560 | tf_op jit(solution)/shard_map/all_gather | solution.py:93
  28.0 8.8 %copy-start.5 = (f32[2,2,128]{2,1,0:T(2,128)S(1)}, f32[2,2,128]{2,1,0:T(2,128)}, u32[]{:S(2)}) copy-start(f32[2,2,128]{2,1,0:T(2,128)} %param.10) | copy-start | bytes 6148
  28.0 9.5 %copy-start.4 = (f32[2,4096]{1,0:T(2,128)S(1)}, f32[2,4096]{1,0:T(2,128)}, u32[]{:S(2)}) copy-start(f32[2,4096]{1,0:T(2,128)} %param.8) | copy-start | bytes 98308
  112.3 3.3 slice-start
  113.4 2.1 slice-start.1
  115.6 7.4 %copy-start.2 = (s32[16,512]{1,0:T(8,128)S(1)}, s32[16,512]{1,0:T(8,128)}, u32[]{:S(2)}) copy-start(s32[16,512]{1,0:T(8,128)} %reshape.311) | copy-start | bytes 98308
  120.6 1.3 copy-start.1
  122.9 94.7 %all-gather.3.cloned.1.call-start = ((), (), s32[]{:S(2)}) async-start(), calls=%async_computation.4 | async-start | bytes 5570560 | tf_op jit(solution)/shard_map/all_gather | solution.py:94
  126.6 198.3 %reduce-scatter.2.cloned.1.call-start = ((), (), s32[]{:S(2)}) async-start(), calls=%async_computation.6 | async-start | bytes 5570560 | tf_op jit(solution)/shard_map/reduce_scatter | solution.py:122
Sparse Core Ops, SparseCore 0:
  22.0 2.4 sort.39.cloned.1.call-done
  244.2 80.6 reduce-scatter.1
  (1 shorter events, 0.0 us)
Sparse Core Ops, SparseCore 1:
  123.0 50.4 all-gather.4
  175.1 42.4 all-gather.2
